TPU v7x, 32 devices: a whole 2x2x4 slice. The times are simulated.
32 devices in a mesh: shard: 8 (over y, x, core), rep: 4 (over z).
Axes of the slice: x: 2, y: 2, z: 4, core: 2. Of those that a mesh axis runs over, the one named last changes fastest.
Arguments:
- tokens: bfloat16 [4, 1024, 1600], P('rep', 'shard'), may hold values from -6 to 6
- segment_ids: int32 [4, 1024], P('rep'), may hold values from 0 to 3, never falling along the last dimension, each value on 1 to 512 neighbouring positions
- ln1_gain: bfloat16 [1600], P('shard'), may hold values from 0.5 to 1.5
- ln1_bias: bfloat16 [1600], P('shard'), may hold values from -2.5 to 2.5
- w_qkv: bfloat16 [1600, 4800], P('shard')
- q_bias: bfloat16 [1600], P('shard'), may hold values from -2.5 to 2.5
- v_bias: bfloat16 [1600], P('shard'), may hold values from -2.5 to 2.5
- w_out: bfloat16 [1600, 1600], P('shard'), may hold values from -0.625 to 0.625
- out_bias: bfloat16 [1600], P('shard'), may hold values from -2.5 to 2.5
- ln2_gain: bfloat16 [1600], P('shard'), may hold values from 0.5 to 1.5
- ln2_bias: bfloat16 [1600], P('shard'), may hold values from -2.5 to 2.5
- w_fc: bfloat16 [1600, 6400], P('shard'), may hold values from -0.15625 to 0.15625
- fc_bias: bfloat16 [6400], P('shard'), may hold values from -2.5 to 2.5
- w_proj: bfloat16 [6400, 1600], P('shard'), may hold values from -0.078125 to 0.078125
- proj_bias: bfloat16 [1600], P('shard'), may hold values from -2.5 to 2.5
- grad_out: bfloat16 [4, 1024, 1600], P('rep', 'shard'), may hold values from -6 to 6
Outputs:
- output: float32 [4, 1024, 1600], P('rep', 'shard')
- grad_tokens: float32 [4, 1024, 1600], P('rep', 'shard')
- grad_ln1_gain: float32 [1600], P('shard')
- grad_ln1_bias: float32 [1600], P('shard')
- grad_w_qkv: float32 [1600, 4800], P('shard', 'rep')
- grad_q_bias: float32 [1600], P('shard')
- grad_v_bias: float32 [1600], P('shard')
- grad_w_out: float32 [1600, 1600], P('shard', 'rep')
- grad_out_bias: float32 [1600], P('shard')
- grad_ln2_gain: float32 [1600], P('shard')
- grad_ln2_bias: float32 [1600], P('shard')
- grad_w_fc: float32 [1600, 6400], P('shard', 'rep')
- grad_fc_bias: float32 [6400], P('shard')
- grad_w_proj: float32 [6400, 1600], P('shard', 'rep')
- grad_proj_bias: float32 [1600], P('shard')
Inputs may be any that keep to these rules, and one draw needn't show every extreme that they name: `segment_ids`: along each sequence the document numbers never fall, and one document covers at most 512 positions.
All inputs are finite; a program needn't handle non-finite values.
Results may differ from a plain program's by a relative error of at most 0.019.
Values may be sent and summed in bfloat16 or wider, within the bound.
No kernel may reach another device: no remote copies, remote signals or barrier semaphores. Data moves between devices by JAX's collectives and lax.ppermute only.
A program may use at most 576 MiB of HBM per device.

v0:
```python
import math
import jax
import jax.numpy as jnp
from jax import lax
from jax.sharding import PartitionSpec as P

HD = 64
EPSILON = 1e-05
GELU_SCALE = math.sqrt(2.0 / math.pi)


def layer_norm(values, gain, shift):
    centre_val = jnp.mean(values, axis=-1, keepdims=True)
    centred = values - centre_val
    variance = jnp.mean(centred * centred, axis=-1, keepdims=True)
    inverse = lax.rsqrt(variance + EPSILON)
    normed = centred * inverse
    return (normed * gain + shift, normed, inverse)


def norm_back(upstream, normed, inverse, gain):
    scaled = upstream * gain
    return inverse * (
        scaled
        - jnp.mean(scaled, axis=-1, keepdims=True)
        - normed * jnp.mean(scaled * normed, axis=-1, keepdims=True)
    )


def gelu_value(inputs_pre):
    cubic = inputs_pre * inputs_pre * inputs_pre
    return 0.5 * inputs_pre * (1.0 + jnp.tanh(GELU_SCALE * (inputs_pre + 0.044715 * cubic)))


def gelu_slope(inputs_pre):
    square = inputs_pre * inputs_pre
    tangent = jnp.tanh(GELU_SCALE * (inputs_pre + 0.044715 * square * inputs_pre))
    return 0.5 * (1.0 + tangent) + 0.5 * inputs_pre * (1.0 - tangent * tangent) * GELU_SCALE * (
        1.0 + 3.0 * 0.044715 * square
    )


def score_table(queries, keys, key_mask, score_scale):
    scores = (
        jnp.einsum("sqhe,skhe->shqk", queries, keys, preferred_element_type=jnp.float32)
        * score_scale
    )
    return jnp.where(key_mask[:, None], scores, -1e30)


def attend(queries, keys, values, key_mask, score_scale):
    scores = score_table(queries, keys, key_mask, score_scale)
    row_max = jnp.max(scores, axis=-1, keepdims=True)
    log_total = row_max + jnp.log(jnp.sum(jnp.exp(scores - row_max), axis=-1, keepdims=True))
    weights_soft = jnp.where(key_mask[:, None], jnp.exp(scores - log_total), 0.0).astype(
        jnp.bfloat16
    )
    mixed = jnp.einsum("shqk,skhe->sqhe", weights_soft, values, preferred_element_type=jnp.float32)
    return (mixed, log_total)


def attend_back(queries, keys, values, key_mask, log_total, grad_mixed, score_scale):
    scores = score_table(queries, keys, key_mask, score_scale)
    weights_soft = jnp.where(key_mask[:, None], jnp.exp(scores - log_total), 0.0)
    grad_soft = jnp.einsum(
        "sqhe,skhe->shqk", grad_mixed, values, preferred_element_type=jnp.float32
    )
    delta = jnp.sum(weights_soft * grad_soft, axis=-1, keepdims=True)
    grad_scores = (weights_soft * (grad_soft - delta) * score_scale).astype(jnp.bfloat16)
    grad_q = jnp.einsum("shqk,skhe->sqhe", grad_scores, keys, preferred_element_type=jnp.float32)
    grad_k = jnp.einsum("shqk,sqhe->skhe", grad_scores, queries, preferred_element_type=jnp.float32)
    grad_v = jnp.einsum(
        "shqk,sqhe->skhe",
        weights_soft.astype(jnp.bfloat16),
        grad_mixed,
        preferred_element_type=jnp.float32,
    )
    return (grad_q, grad_k, grad_v)


def add_rows(operand, shard_rows):
    return jnp.dot(operand, shard_rows, preferred_element_type=jnp.float32)


def back_rows(operand, shard_rows):
    return lax.dot_general(
        operand, shard_rows, (((1,), (1,)), ((), ())), preferred_element_type=jnp.float32
    )


def cross_rows(operand, other):
    return lax.dot_general(
        operand, other, (((0,), (0,)), ((), ())), preferred_element_type=jnp.float32
    )


def local(
    tokens,
    segment_ids,
    ln1_gain,
    ln1_bias,
    w_qkv,
    q_bias,
    v_bias,
    w_out,
    out_bias,
    ln2_gain,
    ln2_bias,
    w_fc,
    fc_bias,
    w_proj,
    proj_bias,
    grad_out,
):
    seq_count, local_len, model_width = tokens.shape
    full_len = segment_ids.shape[1]
    row_count = seq_count * local_len
    head_count = model_width // HD
    score_scale = float(HD) ** (-0.5)
    own_rows = ln1_gain.shape[0]
    hidden_width = w_fc.shape[1]
    fc_ratio = hidden_width // model_width
    own_hidden = own_rows * fc_ratio
    small = (
        lax.all_gather(ln1_gain, "shard", axis=0, tiled=True),
        lax.all_gather(ln1_bias, "shard", axis=0, tiled=True),
        lax.all_gather(q_bias, "shard", axis=0, tiled=True),
        lax.all_gather(v_bias, "shard", axis=0, tiled=True),
        lax.all_gather(out_bias, "shard", axis=0, tiled=True),
        lax.all_gather(ln2_gain, "shard", axis=0, tiled=True),
        lax.all_gather(ln2_bias, "shard", axis=0, tiled=True),
        lax.all_gather(fc_bias, "shard", axis=0, tiled=True),
        lax.all_gather(proj_bias, "shard", axis=0, tiled=True),
    )
    gain_one, shift_one, bias_q, bias_v, bias_out, gain_two, shift_two, bias_fc, bias_proj = [
        member.astype(jnp.float32) for member in small
    ]
    first_pos = lax.axis_index("shard") * local_len
    query_pos = first_pos + jnp.arange(local_len, dtype=jnp.int32)
    key_pos = jnp.arange(full_len, dtype=jnp.int32)
    query_seg = lax.dynamic_slice_in_dim(segment_ids, first_pos, local_len, 1)
    key_mask = (key_pos[None, None, :] <= query_pos[None, :, None]) & (
        query_seg[:, :, None] == segment_ids[:, None, :]
    )
    resid_in = tokens.reshape(row_count, model_width).astype(jnp.float32)
    ln_one, normed_one, inverse_one = layer_norm(resid_in, gain_one, shift_one)
    ln_one_b = ln_one.astype(jnp.bfloat16)
    qkv = add_rows(ln_one_b, lax.all_gather(w_qkv, "shard", axis=0, tiled=True))
    queries = (
        (qkv[:, :model_width] + bias_q)
        .astype(jnp.bfloat16)
        .reshape(seq_count, local_len, head_count, HD)
    )
    key_local = (
        qkv[:, model_width : 2 * model_width]
        .astype(jnp.bfloat16)
        .reshape(seq_count, local_len, model_width)
    )
    value_local = (
        (qkv[:, 2 * model_width :] + bias_v)
        .astype(jnp.bfloat16)
        .reshape(seq_count, local_len, model_width)
    )
    keys_all, values_all = (
        lax.all_gather(key_local, "shard", axis=1, tiled=True),
        lax.all_gather(value_local, "shard", axis=1, tiled=True),
    )
    keys = keys_all.reshape(seq_count, full_len, head_count, HD)
    values = values_all.reshape(seq_count, full_len, head_count, HD)

    def attend_one(items):
        one_q, one_k, one_v, one_mask = items
        one_mixed, one_total = attend(
            one_q[None], one_k[None], one_v[None], one_mask[None], score_scale
        )
        return (one_mixed[0], one_total[0])

    mixed, log_total = lax.map(attend_one, (queries, keys, values, key_mask))
    attended = mixed.reshape(row_count, model_width).astype(jnp.bfloat16)
    attn_proj = add_rows(attended, lax.all_gather(w_out, "shard", axis=0, tiled=True))
    mid = resid_in + attn_proj + bias_out
    ln_two, normed_two, inverse_two = layer_norm(mid, gain_two, shift_two)
    ln_two_b = ln_two.astype(jnp.bfloat16)
    fc_whole, proj_whole = (
        lax.all_gather(w_fc, "shard", axis=0, tiled=True),
        lax.all_gather(w_proj, "shard", axis=0, tiled=True),
    )
    pre_act = jnp.dot(ln_two_b, fc_whole, preferred_element_type=jnp.float32) + bias_fc
    hidden = gelu_value(pre_act).astype(jnp.bfloat16)
    result = mid + jnp.dot(hidden, proj_whole, preferred_element_type=jnp.float32) + bias_proj
    grad_round = grad_out.reshape(row_count, model_width)
    grad_top = grad_round.astype(jnp.float32)
    back_proj, back_fc = (
        lax.all_gather(w_proj, "shard", axis=0, tiled=True),
        lax.all_gather(w_fc, "shard", axis=0, tiled=True),
    )
    grad_hidden = back_rows(grad_round, back_proj)
    grad_pre = grad_hidden * gelu_slope(pre_act)
    grad_pre_round = grad_pre.astype(jnp.bfloat16)
    grad_ln_two = back_rows(grad_pre_round, back_fc)
    grad_mid = grad_top + norm_back(grad_ln_two, normed_two, inverse_two, gain_two)
    grad_mid_round = grad_mid.astype(jnp.bfloat16)
    back_out, back_qkv = (
        lax.all_gather(w_out, "shard", axis=0, tiled=True),
        lax.all_gather(w_qkv, "shard", axis=0, tiled=True),
    )
    grad_attn = back_rows(grad_mid_round, back_out)
    grad_attended = grad_attn.astype(jnp.bfloat16).reshape(seq_count, local_len, head_count, HD)

    def attend_one_back(items):
        one_q, one_k, one_v, one_mask, one_total, one_grad = items
        part_q, part_k, part_v = attend_back(
            one_q[None],
            one_k[None],
            one_v[None],
            one_mask[None],
            one_total[None],
            one_grad[None],
            score_scale,
        )
        return (part_q[0], part_k[0], part_v[0])

    grad_q, grad_k_all, grad_v_all = lax.map(
        attend_one_back, (queries, keys, values, key_mask, log_total, grad_attended)
    )
    grad_k_own, grad_v_own = (
        lax.psum_scatter(
            grad_k_all.reshape(seq_count, full_len, model_width).astype(jnp.bfloat16),
            "shard",
            scatter_dimension=1,
            tiled=True,
        ).astype(jnp.float32),
        lax.psum_scatter(
            grad_v_all.reshape(seq_count, full_len, model_width).astype(jnp.bfloat16),
            "shard",
            scatter_dimension=1,
            tiled=True,
        ).astype(jnp.float32),
    )
    grad_q = grad_q.reshape(row_count, model_width)
    grad_k_own = grad_k_own.reshape(row_count, model_width)
    grad_v_own = grad_v_own.reshape(row_count, model_width)
    grad_qkv = jnp.concatenate([grad_q, grad_k_own, grad_v_own], axis=1).astype(jnp.bfloat16)
    grad_ln_one = back_rows(grad_qkv, back_qkv)
    grad_in = grad_mid + norm_back(grad_ln_one, normed_one, inverse_one, gain_one)
    small_cols = jnp.concatenate(
        [
            jnp.stack(
                [
                    jnp.sum(grad_ln_one * normed_one, axis=0),
                    jnp.sum(grad_ln_one, axis=0),
                    jnp.sum(grad_q, axis=0),
                    jnp.sum(grad_v_own, axis=0),
                    jnp.sum(grad_mid, axis=0),
                    jnp.sum(grad_ln_two * normed_two, axis=0),
                    jnp.sum(grad_ln_two, axis=0),
                    jnp.sum(grad_top, axis=0),
                ],
                axis=1,
            ),
            jnp.sum(grad_pre, axis=0).reshape(model_width, fc_ratio),
            jnp.zeros((model_width, 128 - 8 - fc_ratio), jnp.float32),
        ],
        axis=1,
    )
    part_qkv = cross_rows(ln_one_b, grad_qkv)
    part_out = cross_rows(attended, grad_mid_round)
    part_fc = cross_rows(ln_two_b, grad_pre_round)
    part_proj = cross_rows(hidden, grad_round).reshape(
        own_rows * lax.axis_size("shard"), fc_ratio * model_width
    )
    owned = lax.psum_scatter(
        jnp.concatenate([part_qkv, part_out, part_fc, part_proj, small_cols], axis=1).astype(
            jnp.bfloat16
        ),
        "shard",
        scatter_dimension=0,
        tiled=True,
    ).astype(jnp.float32)
    base = 4 * model_width + hidden_width + fc_ratio * model_width
    parts = (
        owned[:, : 3 * model_width],
        owned[:, 3 * model_width : 4 * model_width],
        owned[:, 4 * model_width : 4 * model_width + hidden_width],
        owned[:, 4 * model_width + hidden_width : base].reshape(own_hidden, model_width),
    )
    small_own = owned[:, base:]
    total_qkv, total_out, total_fc, total_proj = (
        lax.psum_scatter(
            parts[0].astype(jnp.bfloat16), "rep", scatter_dimension=1, tiled=True
        ).astype(jnp.float32),
        lax.psum_scatter(
            parts[1].astype(jnp.bfloat16), "rep", scatter_dimension=1, tiled=True
        ).astype(jnp.float32),
        lax.psum_scatter(
            parts[2].astype(jnp.bfloat16), "rep", scatter_dimension=1, tiled=True
        ).astype(jnp.float32),
        lax.psum_scatter(
            parts[3].astype(jnp.bfloat16), "rep", scatter_dimension=1, tiled=True
        ).astype(jnp.float32),
    )
    total_small = lax.psum(small_own.astype(jnp.bfloat16), "rep").astype(jnp.float32)
    return (
        result.reshape(seq_count, local_len, model_width),
        grad_in.reshape(seq_count, local_len, model_width),
        total_small[:, 0],
        total_small[:, 1],
        total_qkv,
        total_small[:, 2],
        total_small[:, 3],
        total_out,
        total_small[:, 4],
        total_small[:, 5],
        total_small[:, 6],
        total_fc,
        total_small[:, 8 : 8 + fc_ratio].reshape(own_hidden),
        total_proj,
        total_small[:, 7],
    )


def solution(mesh):
    return jax.shard_map(
        local,
        mesh=mesh,
        in_specs=(
            P("rep", "shard", None),
            P("rep", None),
            P("shard"),
            P("shard"),
            P("shard", None),
            P("shard"),
            P("shard"),
            P("shard", None),
            P("shard"),
            P("shard"),
            P("shard"),
            P("shard", None),
            P("shard"),
            P("shard", None),
            P("shard"),
            P("rep", "shard", None),
        ),
        out_specs=(
            P("rep", "shard", None),
            P("rep", "shard", None),
            P("shard"),
            P("shard"),
            P("shard", "rep"),
            P("shard"),
            P("shard"),
            P("shard", "rep"),
            P("shard"),
            P("shard"),
            P("shard"),
            P("shard", "rep"),
            P("shard"),
            P("shard", "rep"),
            P("shard"),
        ),
        check_vma=False,
    )
```

profile of v0, /device:TPU:0, one launch (start us, length us, event | category | flops | bytes accessed | tf_op | source)
XLA Modules:
  0.0 1772.5 jit_solution(15159649565087665562)
XLA Ops:
  18.3 29.0 %all-reduce.10 = (bf16[1600]{0:T(1024)(128)(2,1)S(1)}, bf16[1600]{0:T(1024)(128)(2,1)S(1)}, bf16[1600]{0:T(1024)(128)(2,1)S(1)}, bf16[1600]{0:T(1024)(128)(2,1)S...) all-reduce(bf16[1600]{0:T(1024)(128)(2,1)S(1)} %dynamic-update-slic, ...), channel_id=1, replica_groups=mesh['shard'=8,'rep'=4] {'shard'}, use_global_device_ids=true, to_apply=%add.1 | all-reduce | flops 19200 | bytes 76800
  49.7 48.3 %all-gather.9.cloned.1.call-done = bf16[1600,4800]{1,0:T(8,128)(2,1)} async-done(((bf16[200,4800]{1,0:T(8,128)(2,1)}), bf16[1600,4800]{1,0:T(8,128)(2,1)}) %all-gather.9.cloned.1.call-update) | async-done | bytes 15360016 | tf_op jit(solution)/shard_map/all_gather | solution.py:148
  113.0 29.8 %all-gather.19.cloned.1.call-done = bf16[1024,1600]{0,1:T(8,128)(2,1)} async-done(((bf16[128,1600]{0,1:T(8,128)(2,1)}), bf16[1024,1600]{0,1:T(8,128)(2,1)}) %all-gather.19.cloned.1.call-update) | async-done | bytes 3276816 | tf_op jit(solution)/shard_map/all_gather | solution.py:165
  151.8 26.8 %all-gather.17.cloned.1.call-done = bf16[1024,1600]{0,1:T(8,128)(2,1)} async-done(((bf16[128,1600]{0,1:T(8,128)(2,1)}), bf16[1024,1600]{0,1:T(8,128)(2,1)}) %all-gather.17.cloned.1.call-update) | async-done | bytes 3276816 | tf_op jit(solution)/shard_map/all_gather | solution.py:166
  187.0 34.7 %all-gather.11.cloned.1.call-done = bf16[1600,1600]{1,0:T(8,128)(2,1)} async-done(((bf16[200,1600]{1,0:T(8,128)(2,1)}), bf16[1600,1600]{1,0:T(8,128)(2,1)}) %all-gather.11.cloned.1.call-update) | async-done | bytes 5120016 | tf_op jit(solution)/shard_map/all_gather | solution.py:180
  226.8 102.1 %all-gather.13.cloned.1.call-done = bf16[1600,6400]{1,0:T(8,128)(2,1)} async-done(((bf16[200,6400]{1,0:T(8,128)(2,1)}), bf16[1600,6400]{1,0:T(8,128)(2,1)}) %all-gather.13.cloned.1.call-update) | async-done | bytes 20480016 | tf_op jit(solution)/shard_map/all_gather | solution.py:185
  328.8 12.4 convolution_add_fusion
  341.2 98.2 %all-gather.15.cloned.1.call-done = bf16[6400,1600]{1,0:T(8,128)(2,1)} async-done(((bf16[800,1600]{1,0:T(8,128)(2,1)}), bf16[6400,1600]{1,0:T(8,128)(2,1)}) %all-gather.15.cloned.1.call-update) | async-done | bytes 20480016 | tf_op jit(solution)/shard_map/all_gather | solution.py:186
  439.5 12.4 fusion.99
  451.9 12.1 multiply_reduce_fusion.1
  473.5 16.2 copy.55
  505.2 33.4 %fusion.40 = bf16[25,64,1024]{2,1,0:T(8,128)(2,1)} fusion(bf16[128,25,64]{0,2,1:T(8,128)(2,1)S(1)} %bitcast.144, f32[25,128,1024]{2,1,0:T(8,128)} %fusion.100, f32[25,128,1024]{2,1,0:T(8,128)} %copy-done, f32[25,128]{1,0:T(8,128)S(1)} %log_add_fusion, pred[128,1024]{1,0:T(8,128)(4,1)S(1)} %fusion.69), kind=kOutput, calls=%fused_computation.48 | convolution fusion | flops 450564224 | bytes 30044672 | tf_op jit(solution)/shard_map/while/body/eval_jaxpr/shqk,sqhe->skhe/dot_general | solution.py:71
  538.6 16.3 copy.53
  561.6 12.7 convolution_convert_fusion
  574.3 30.6 %copy.43 = bf16[6400,1600]{1,0:T(8,128)(2,1)} copy(bf16[6400,1600]{0,1:T(8,128)(2,1)} %convolution_convert_fusion) | data formatting | bytes 40960000 | tf_op jit(solution)/shard_map/convert.29
  605.0 35.8 %reshape.340 = bf16[1600,6400]{1,0:T(8,128)(2,1)} reshape(bf16[6400,1600]{1,0:T(8,128)(2,1)} %copy.43) | data formatting | bytes 40960000 | tf_op jit(solution)/shard_map/reshape | solution.py:269
  640.8 33.8 %fusion.93 = (bf16[25,64]{1,0:T(8,128)(2,1)S(1)}, bf16[1,128,25,64]{1,3,2,0:T(8,128)(2,1)}) fusion(bf16[1024,25,64]{0,2,1:T(8,128)(2,1)} %bitcast.138, f32[25,128,1024]{2,1,0:T(8,128)} %fusion.100, f32[25,128,1024]{2,1,0:T(8,128)} %copy-done, f32[25,128]{1,0:T(8,128)S(1)} %log_add_fusion, pred[128,1024]{1,0:T(8,128)(4,1)S(1)} %fusion.69), kind=kOutput, calls=%fused_computation.128 | convolution fusion | flops 449333824 | bytes 30047872 | tf_op jit(solution)/shard_map/while/body/eval_jaxpr/shqk,skhe->sqhe/dot_general | solution.py:70
  714.8 10.9 fusion.62
  729.6 130.5 %concatenate.9 = bf16[1600,19328]{1,0:T(8,128)(2,1)} concatenate(bf16[1600,4800]{1,0:T(8,128)(2,1)} %convolution_convert_fusion.2, bf16[1600,1600]{1,0:T(8,128)(2,1)} %convolution_convert_fusion.3, bf16[1600,6400]{1,0:T(8,128)(2,1)} %convolution_convert_fusion.1, bf16[1600,6400]{1,0:T(8,128)(2,1)} %reshape.340, bf16[1600,1]{1,0:T(8,128)(2,1)} %stack.40, bf16[1600,1]{1,0:T(8,128)(2,1)} %stack.41, ...), dimensions={1} | concatenate | bytes 123699200 | tf_op jit(solution)/shard_map/concatenate | solution.py:273
  860.9 699.7 %all-reduce.13.cloned.1.call-done = bf16[1600,19328]{1,0:T(8,128)(2,1)} async-done(((bf16[1600,19328]{1,0:T(8,128)(2,1)}), bf16[1600,19328]{1,0:T(8,128)(2,1)}) %all-reduce.13.cloned.1.call-update) | async-done | bytes 61849616
  1593.5 15.0 fusion.39
  1611.8 22.2 %psum.7 = bf16[200,128]{1,0:T(8,128)(2,1)S(1)} all-reduce(bf16[200,128]{1,0:T(8,128)(2,1)S(1)} %dynamic-slice.11), channel_id=1, replica_groups=mesh['shard'=8,'rep'=4] {'rep'}, use_global_device_ids=true, to_apply=%region_23.24 | all-reduce | flops 25600 | bytes 102400 | tf_op jit(solution)/shard_map/psum | solution.py:302
  1642.8 61.9 %reduce-scatter.27.cloned.1.call-done = bf16[1600,200]{1,0:T(8,128)(2,1)} async-done(((bf16[6400,200]{1,0:T(8,128)(2,1)}), bf16[1600,200]{1,0:T(8,128)(2,1)}) %reduce-scatter.27.cloned.1.call-update) | async-done | bytes 640016
  1707.3 55.9 %reduce-scatter.17.cloned.1.call-done = bf16[800,400]{0,1:T(8,128)(2,1)} async-done(((bf16[800,1600]{0,1:T(8,128)(2,1)}), bf16[800,400]{0,1:T(8,128)(2,1)}) %reduce-scatter.17.cloned.1.call-update) | async-done | bytes 640016 | tf_op jit(solution)/shard_map/reduce_scatter | solution.py:298
  (165 shorter events, 175.0 us)
Async XLA Ops:
  7.2 90.9 %all-gather.9.cloned.1.call-start = ((), (), s32[]{:S(2)}) async-start(), calls=%async_computation.6 | async-start | bytes 17510400 | tf_op jit(solution)/shard_map/all_gather | solution.py:148
  7.9 134.9 %all-gather.19.cloned.1.call-start = ((), (), s32[]{:S(2)}) async-start(), calls=%async_computation.12 | async-start | bytes 3686400 | tf_op jit(solution)/shard_map/all_gather | solution.py:165
  109.4 69.2 %all-gather.17.cloned.1.call-start = ((), (), s32[]{:S(2)}) async-start(), calls=%async_computation.11 | async-start | bytes 3686400 | tf_op jit(solution)/shard_map/all_gather | solution.py:166
  110.7 36.5 %copy-start.11 = (bf16[128,1600]{0,1:T(8,128)(2,1)}, bf16[128,1600]{0,1:T(8,128)(2,1)S(1)}, u32[]{:S(2)}) copy-start(bf16[128,1600]{0,1:T(8,128)(2,1)S(1)} %get-tuple-element.97) | copy-start | bytes 1228804
  110.7 111.0 %all-gather.11.cloned.1.call-start = ((), (), s32[]{:S(2)}) async-start(), calls=%async_computation.7 | async-start | bytes 5990400 | tf_op jit(solution)/shard_map/all_gather | solution.py:180
  111.3 217.6 %all-gather.13.cloned.1.call-start = ((), (), s32[]{:S(2)}) async-start(), calls=%async_computation.8 | async-start | bytes 23040000 | tf_op jit(solution)/shard_map/all_gather | solution.py:185
  111.8 327.6 %all-gather.15.cloned.1.call-start = ((), (), s32[]{:S(2)}) async-start(), calls=%async_computation.9 | async-start | bytes 23961600 | tf_op jit(solution)/shard_map/all_gather | solution.py:186
  112.4 582.1 %reduce-scatter.21.cloned.1.call-start = ((), (), s32[]{:S(2)}) async-start(), calls=%async_computation.14 | async-start | bytes 3833856
  178.6 43.1 %copy-start.1 = (bf16[1,128,1600]{1,2,0:T(8,128)(2,1)S(1)}, bf16[1,128,1600]{1,2,0:T(8,128)(2,1)}, u32[]{:S(2)}) copy-start(bf16[1,128,1600]{1,2,0:T(8,128)(2,1)} %param.16) | copy-start | bytes 1228804
  186.9 39.6 %copy-start.8 = (bf16[25,64,128]{2,1,0:T(8,128)(2,1)}, bf16[25,64,128]{2,1,0:T(8,128)(2,1)S(1)}, u32[]{:S(2)}) copy-start(bf16[25,64,128]{2,1,0:T(8,128)(2,1)S(1)} %convolution_convert_fusion.6) | copy-start | bytes 1228804
  226.8 212.7 %copy-start.5 = (bf16[1,128,1600]{1,2,0:T(8,128)(2,1)S(1)}, bf16[1,128,1600]{1,2,0:T(8,128)(2,1)}, u32[]{:S(2)}) copy-start(bf16[1,128,1600]{1,2,0:T(8,128)(2,1)} %param.31) | copy-start | bytes 1228804
  439.5 29.5 %slice-start = ((s8[13107200]{0:T(1024)(128)(4,1)}), s8[4194304]{0:T(1024)(128)(4,1)S(1)}, s32[]{:S(2)}) async-start(s8[13107200]{0:T(1024)(128)(4,1)} %bitcast.124), calls=%async_computation.19 | async-start | bytes 8388608
  439.5 29.5 %slice-start.1 = ((s8[13107200]{0:T(1024)(128)(4,1)}), s8[524288]{0:T(1024)(128)(4,1)S(1)}, s32[]{:S(2)}) async-start(s8[13107200]{0:T(1024)(128)(4,1)} %bitcast.124), calls=%async_computation.20 | async-start | bytes 1048576
  451.9 17.1 slice-start.2
  451.9 17.1 slice-start.3
  495.1 205.0 %reduce-scatter.19.cloned.1.call-start = ((), (), s32[]{:S(2)}) async-start(), calls=%async_computation.13 | async-start | bytes 3833856
  560.1 1000.5 %all-reduce.13.cloned.1.call-start = ((), (), s32[]{:S(2)}) async-start(), calls=%async_computation.18 | async-start | bytes 123699200
  640.8 39.4 %copy-start.3 = (f32[128,1600]{0,1:T(8,128)S(1)}, f32[128,1600]{0,1:T(8,128)}, u32[]{:S(2)}) copy-start(f32[128,1600]{0,1:T(8,128)} %copy-done.2) | copy-start | bytes 2457604
  640.8 39.4 %copy-start.9 = (bf16[25,64,128]{2,1,0:T(8,128)(2,1)S(1)}, bf16[25,64,128]{2,1,0:T(8,128)(2,1)}, u32[]{:S(2)}) copy-start(bf16[25,64,128]{2,1,0:T(8,128)(2,1)} %copy-done.8) | copy-start | bytes 1228804
  714.8 14.8 copy-start.10
  860.2 775.8 %reduce-scatter.25.cloned.1.call-start = ((), (), s32[]{:S(2)}) async-start(), calls=%async_computation.16 | async-start | bytes 1024000
  1563.2 77.3 %reduce-scatter.23.cloned.1.call-start = ((), (), s32[]{:S(2)}) async-start(), calls=%async_computation.15 | async-start | bytes 3072000
  1570.4 134.3 %reduce-scatter.27.cloned.1.call-start = ((), (), s32[]{:S(2)}) async-start(), calls=%async_computation.17 | async-start | bytes 4096000
  1582.4 180.9 %reduce-scatter.17.cloned.1.call-start = ((), (), s32[]{:S(2)}) async-start(), calls=%async_computation.10 | async-start | bytes 3584000 | tf_op jit(solution)/shard_map/reduce_scatter | solution.py:298
  (9 other events, 41.5 us)
Sparse Core Ops, SparseCore 0:
  9.9 88.1 all-gather.8
  109.5 33.2 all-gather.18
  145.3 33.2 all-gather.16
  180.3 41.3 all-gather.10
  223.4 105.3 all-gather.12
  330.6 108.8 all-gather.14
  495.2 47.4 reduce-scatter.20
  560.2 47.4 reduce-scatter.18
  860.3 700.2 all-reduce.12
  1563.3 23.7 reduce-scatter.24
  1589.4 50.9 reduce-scatter.22
  1642.6 62.0 reduce-scatter.26
  1707.0 56.2 reduce-scatter.16
where the time goes:
time: 1790 us; the launch traced here: 1770 us
  waiting for transfers between devices  1160 us (65%)
  local copies, waits for them, and re-layouts  311 us (17%)
  matrix products  213 us (12%)
  blocking collectives  51.2 us (3%)
    unnamed x19, waiting for transfers between devices  767 us
    concatenate x1, local copies, waits for them, and re-layouts, local(): jnp.concatenate([part_qkv, part_out, part_fc, part_proj, small_cols], axi...  131 us
    all_gather x1, waiting for transfers between devices, local(): lax.all_gather(w_fc, 'shard', axis=0, tiled=True)  102 us
    all_gather x1, waiting for transfers between devices, local(): lax.all_gather(w_proj, 'shard', axis=0, tiled=True)  98.2 us
    unnamed x72, local copies, waits for them, and re-layouts  76.8 us
    reduce_scatter x1, waiting for transfers between devices, local(): lax.psum_scatter(parts[3].astype(jnp.bfloat16), 'rep', scatter_dimension=...  55.9 us
    all_gather x1, waiting for transfers between devices, local(): qkv = add_rows(ln_one_b, lax.all_gather(w_qkv, 'shard', axis=0, tiled=True))  48.3 us
    dot_general x4, matrix products, back_rows(): lax.dot_general(operand, shard_rows, (((1,), (1,)), ((), ())), preferred_...  39.8 us
  transfers between devices with their start and end apart: 13, of which 10 were waited for; matrix products, arithmetic and copies ran while one was open for 17% of the time, Pallas kernels for 0%

commit v1 on v0

--- a/solution.py
+++ b/solution.py
@@ -7,6 +7,22 @@
 HD = 64
 EPSILON = 1e-05
 GELU_SCALE = math.sqrt(2.0 / math.pi)
+
+
+def gather_around(x, axis, dim):
+    ways, here, step = (lax.axis_size(axis), lax.axis_index(axis), x.shape[dim])
+    dims = [n * ways if d == dim else n for d, n in enumerate(x.shape)]
+    full = lax.dynamic_update_slice_in_dim(jnp.zeros(dims, x.dtype), x, here * step, axis=dim)
+    going_up = going_down = x
+    for far in range(1, ways // 2 + 1):
+        going_up = lax.ppermute(going_up, axis, [(d, (d + 1) % ways) for d in range(ways)])
+        full = lax.dynamic_update_slice_in_dim(full, going_up, (here - far) % ways * step, axis=dim)
+        if 2 * far < ways:
+            going_down = lax.ppermute(going_down, axis, [(d, (d - 1) % ways) for d in range(ways)])
+            full = lax.dynamic_update_slice_in_dim(
+                full, going_down, (here + far) % ways * step, axis=dim
+            )
+    return full
 
 
 def layer_norm(values, gain, shift):
@@ -182,7 +198,7 @@
     ln_two, normed_two, inverse_two = layer_norm(mid, gain_two, shift_two)
     ln_two_b = ln_two.astype(jnp.bfloat16)
     fc_whole, proj_whole = (
-        lax.all_gather(w_fc, "shard", axis=0, tiled=True),
+        gather_around(w_fc, "shard", 0),
         lax.all_gather(w_proj, "shard", axis=0, tiled=True),
     )
     pre_act = jnp.dot(ln_two_b, fc_whole, preferred_element_type=jnp.float32) + bias_fc

time: 1790 us -> 1890 us (1.056)
  waiting for transfers between devices: 1160 us -> 1210 us
  local copies, waits for them, and re-layouts: 311 us -> 335 us
    ppermute x0 -> x7, waiting for transfers between devices: none -> 299 us  [the longest x4 288 us: gather_around(): lax.ppermute(going_up, axis, [(d, (d + 1) % ways) for d in range(ways)])]
    all_gather x1, waiting for transfers between devices: 98.2 us -> 0.01 us  [local(): lax.all_gather(w_proj, 'shard', axis=0, tiled=True)]
    all_gather x1, waiting for transfers between devices: 102 us -> 41.3 us  [local(): lax.all_gather(w_fc, 'shard', axis=0, tiled=True)]
    all_gather x1, waiting for transfers between devices: 34.7 us -> 0.02 us  [local(): lax.all_gather(w_out, 'shard', axis=0, tiled=True)]
    all_gather x1, waiting for transfers between devices: 29.8 us -> 0.01 us  [local(): lax.all_gather(key_local, 'shard', axis=1, tiled=True)]
    all_gather x1, waiting for transfers between devices: 26.8 us -> 0.02 us  [local(): lax.all_gather(value_local, 'shard', axis=1, tiled=True)]
    dynamic_update_slice x0 -> x8, local copies, waits for them, and re-layouts: none -> 19.7 us  [the longest x4 10.6 us: gather_around(): lax.dynamic_update_slice_in_dim(full, going_up, (here - far) % ways * ste...]
    unnamed x72 -> x86, local copies, waits for them, and re-layouts: 76.8 us -> 73.5 us
  transfers between devices with their start and end apart: 13 -> 20, of which waited for: 10 -> 12; matrix products, arithmetic and copies ran while one was open for 17% -> 19% of each run, Pallas kernels for 0% -> 0%
where the time goes in v1:
time: 1890 us; the launch traced here: 1870 us
  waiting for transfers between devices  1210 us (64%)
  local copies, waits for them, and re-layouts  335 us (18%)
  matrix products  226 us (12%)
  blocking collectives  51.2 us (3%)
    unnamed x19, waiting for transfers between devices  768 us
    ppermute x4, waiting for transfers between devices, gather_around(): lax.ppermute(going_up, axis, [(d, (d + 1) % ways) for d in range(ways)])  288 us
    concatenate x1, local copies, waits for them, and re-layouts, local(): jnp.concatenate([part_qkv, part_out, part_fc, part_proj, small_cols], axi...  130 us
    unnamed x86, local copies, waits for them, and re-layouts  73.5 us
    reduce_scatter x1, waiting for transfers between devices, local(): lax.psum_scatter(parts[3].astype(jnp.bfloat16), 'rep', scatter_dimension=...  55.9 us
    all_gather x1, waiting for transfers between devices, local(): qkv = add_rows(ln_one_b, lax.all_gather(w_qkv, 'shard', axis=0, tiled=True))  48.3 us
    all_gather x1, waiting for transfers between devices, local(): lax.all_gather(w_fc, 'shard', axis=0, tiled=True)  41.3 us
    dot_general x4, matrix products, back_rows(): lax.dot_general(operand, shard_rows, (((1,), (1,)), ((), ())), preferred_...  38 us
  transfers between devices with their start and end apart: 20, of which 12 were waited for; matrix products, arithmetic and copies ran while one was open for 19% of the time, Pallas kernels for 0%

profile of v1, /device:TPU:0, one launch (start us, length us, event | category | flops | bytes accessed | tf_op | source)
XLA Modules:
  0.0 1868.5 jit_solution(11149643619965822903)
XLA Ops:
  18.3 29.0 %all-reduce.10 = (bf16[1600]{0:T(1024)(128)(2,1)S(1)}, bf16[1600]{0:T(1024)(128)(2,1)S(1)}, bf16[1600]{0:T(1024)(128)(2,1)S(1)}, bf16[1600]{0:T(1024)(128)(2,1)S...) all-reduce(bf16[1600]{0:T(1024)(128)(2,1)S(1)} %dynamic-update-slic, ...), channel_id=1, replica_groups=mesh['shard'=8,'rep'=4] {'shard'}, use_global_device_ids=true, to_apply=%add.1 | all-reduce | flops 19200 | bytes 76800
  49.7 48.3 %all-gather.9.cloned.1.call-done = bf16[1600,4800]{1,0:T(8,128)(2,1)} async-done(((bf16[200,4800]{1,0:T(8,128)(2,1)}), bf16[1600,4800]{1,0:T(8,128)(2,1)}) %all-gather.9.cloned.1.call-update) | async-done | bytes 15360016 | tf_op jit(solution)/shard_map/all_gather | solution.py:164
  98.0 13.7 fusion.87
  121.0 76.8 %collective-permute-done = bf16[200,6400]{1,0:T(8,128)(2,1)} collective-permute-done((bf16[200,6400]{1,0:T(8,128)(2,1)S(1)}, bf16[200,6400]{1,0:T(8,128)(2,1)}, u32[]{:S(2)}, u32[]{:S(2)}) %collective-permute-start) | collective-permute-done | bytes 2560032 | tf_op jit(solution)/shard_map/ppermute | solution.py:18
  212.4 66.9 %collective-permute-done.2 = bf16[200,6400]{1,0:T(8,128)(2,1)} collective-permute-done((bf16[200,6400]{1,0:T(8,128)(2,1)}, bf16[200,6400]{1,0:T(8,128)(2,1)}, u32[]{:S(2)}, u32[]{:S(2)}) %collective-permute-start.2) | collective-permute-done | bytes 2560032 | tf_op jit(solution)/shard_map/ppermute | solution.py:18
  293.1 84.9 %collective-permute-done.4 = bf16[200,6400]{1,0:T(8,128)(2,1)S(1)} collective-permute-done((bf16[200,6400]{1,0:T(8,128)(2,1)}, bf16[200,6400]{1,0:T(8,128)(2,1)S(1)}, u32[]{:S(2)}, u32[]{:S(2)}) %collective-permute-start.4) | collective-permute-done | bytes 2560032 | tf_op jit(solution)/shard_map/ppermute | solution.py:18
  391.4 59.8 %collective-permute-done.6 = bf16[200,6400]{1,0:T(8,128)(2,1)S(1)} collective-permute-done((bf16[200,6400]{1,0:T(8,128)(2,1)S(1)}, bf16[200,6400]{1,0:T(8,128)(2,1)S(1)}, u32[]{:S(2)}, u32[]{:S(2)}) %collective-permute-start.6) | collective-permute-done | bytes 2560032 | tf_op jit(solution)/shard_map/ppermute | solution.py:18
  476.4 23.8 %convolution_add_fusion = f32[128,6400]{1,0:T(8,128)} fusion(bf16[1600,6400]{1,0:T(8,128)(2,1)} %constant_dynamic-update-slice_fusion, f32[6400]{0:T(1024)S(1)} %convert_element_type.174, f32[128,1600]{0,1:T(8,128)S(1)} %get-tuple-element.106, f32[1600]{0:T(1024)S(1)} %convert_element_type.172, f32[1600]{0:T(1024)S(1)} %convert_element_type.171, ...), kind=kOutput, calls=%fused_computation.11 | convolution fusion | flops 2623283200 | bytes 24615424 | tf_op jit(solution)/shard_map/dot_general | solution.py:204
  500.2 11.4 fusion.100
  511.6 41.3 %all-gather.15.cloned.1.call-done = bf16[1600,6400]{1,0:T(8,128)(2,1)} async-done(((bf16[200,6400]{1,0:T(8,128)(2,1)}), bf16[1600,6400]{1,0:T(8,128)(2,1)}) %all-gather.15.cloned.1.call-update) | async-done | bytes 20480016 | tf_op jit(solution)/shard_map/all_gather | solution.py:211
  552.9 11.7 multiply_reduce_fusion.1
  573.8 16.2 copy.55
  604.6 33.4 %fusion.40 = bf16[25,64,1024]{2,1,0:T(8,128)(2,1)} fusion(bf16[128,25,64]{0,2,1:T(8,128)(2,1)S(1)} %bitcast.144, f32[25,128,1024]{2,1,0:T(8,128)} %fusion.101, f32[25,128,1024]{2,1,0:T(8,128)} %copy-done, f32[25,128]{1,0:T(8,128)S(1)} %log_add_fusion, pred[128,1024]{1,0:T(8,128)(4,1)S(1)} %fusion.69), kind=kOutput, calls=%fused_computation.48 | convolution fusion | flops 450564224 | bytes 30044672 | tf_op jit(solution)/shard_map/while/body/eval_jaxpr/shqk,sqhe->skhe/dot_general | solution.py:87
  638.0 16.3 copy.53
  661.2 12.6 convolution_convert_fusion
  673.8 30.7 %copy.43 = bf16[6400,1600]{1,0:T(8,128)(2,1)} copy(bf16[6400,1600]{0,1:T(8,128)(2,1)} %convolution_convert_fusion) | data formatting | bytes 40960000 | tf_op jit(solution)/shard_map/convert.29
  704.5 35.8 %reshape.340 = bf16[1600,6400]{1,0:T(8,128)(2,1)} reshape(bf16[6400,1600]{1,0:T(8,128)(2,1)} %copy.43) | data formatting | bytes 40960000 | tf_op jit(solution)/shard_map/reshape | solution.py:285
  740.3 33.8 %fusion.94 = (bf16[25,64]{1,0:T(8,128)(2,1)S(1)}, bf16[1,128,25,64]{1,3,2,0:T(8,128)(2,1)}) fusion(bf16[1024,25,64]{0,2,1:T(8,128)(2,1)} %bitcast.138, f32[25,128,1024]{2,1,0:T(8,128)} %fusion.101, f32[25,128,1024]{2,1,0:T(8,128)} %copy-done, f32[25,128]{1,0:T(8,128)S(1)} %log_add_fusion, pred[128,1024]{1,0:T(8,128)(4,1)S(1)} %fusion.69), kind=kOutput, calls=%fused_computation.137 | convolution fusion | flops 449333824 | bytes 30047872 | tf_op jit(solution)/shard_map/while/body/eval_jaxpr/shqk,skhe->sqhe/dot_general | solution.py:86
  825.8 130.1 %concatenate.9 = bf16[1600,19328]{1,0:T(8,128)(2,1)} concatenate(bf16[1600,4800]{1,0:T(8,128)(2,1)} %convolution_convert_fusion.2, bf16[1600,1600]{1,0:T(8,128)(2,1)} %convolution_convert_fusion.3, bf16[1600,6400]{1,0:T(8,128)(2,1)} %convolution_convert_fusion.1, bf16[1600,6400]{1,0:T(8,128)(2,1)} %reshape.340, bf16[1600,1]{1,0:T(8,128)(2,1)} %stack.40, bf16[1600,1]{1,0:T(8,128)(2,1)} %stack.41, ...), dimensions={1} | concatenate | bytes 123699200 | tf_op jit(solution)/shard_map/concatenate | solution.py:289
  956.6 700.0 %all-reduce.13.cloned.1.call-done = bf16[1600,19328]{1,0:T(8,128)(2,1)} async-done(((bf16[1600,19328]{1,0:T(8,128)(2,1)}), bf16[1600,19328]{1,0:T(8,128)(2,1)}) %all-reduce.13.cloned.1.call-update) | async-done | bytes 61849616
  1689.8 15.0 fusion.39
  1707.0 22.3 %psum.7 = bf16[200,128]{1,0:T(8,128)(2,1)S(1)} all-reduce(bf16[200,128]{1,0:T(8,128)(2,1)S(1)} %dynamic-slice.11), channel_id=1, replica_groups=mesh['shard'=8,'rep'=4] {'rep'}, use_global_device_ids=true, to_apply=%region_23.24 | all-reduce | flops 25600 | bytes 102400 | tf_op jit(solution)/shard_map/psum | solution.py:318
  1739.0 61.7 %reduce-scatter.27.cloned.1.call-done = bf16[1600,200]{1,0:T(8,128)(2,1)} async-done(((bf16[6400,200]{1,0:T(8,128)(2,1)}), bf16[1600,200]{1,0:T(8,128)(2,1)}) %reduce-scatter.27.cloned.1.call-update) | async-done | bytes 640016
  1803.3 55.9 %reduce-scatter.17.cloned.1.call-done = bf16[800,400]{0,1:T(8,128)(2,1)} async-done(((bf16[800,1600]{0,1:T(8,128)(2,1)}), bf16[800,400]{0,1:T(8,128)(2,1)}) %reduce-scatter.17.cloned.1.call-update) | async-done | bytes 640016 | tf_op jit(solution)/shard_map/reduce_scatter | solution.py:314
  (202 shorter events, 220.5 us)
Async XLA Ops:
  7.2 90.9 %all-gather.9.cloned.1.call-start = ((), (), s32[]{:S(2)}) async-start(), calls=%async_computation.6 | async-start | bytes 17510400 | tf_op jit(solution)/shard_map/all_gather | solution.py:164
  7.9 444.9 %all-gather.19.cloned.1.call-start = ((), (), s32[]{:S(2)}) async-start(), calls=%async_computation.12 | async-start | bytes 3686400 | tf_op jit(solution)/shard_map/all_gather | solution.py:181
  47.2 50.8 %copy-start.15 = (f32[1600]{0:T(1024)}, f32[1600]{0:T(1024)S(1)}, u32[]{:S(2)}) copy-start(f32[1600]{0:T(1024)S(1)} %convert_element_type.159) | copy-start | bytes 19204
  111.7 86.3 %copy-start.21 = (s32[1,1024]{1,0:T(1,128)S(1)}, s32[1,1024]{1,0:T(1,128)}, u32[]{:S(2)}) copy-start(s32[1,1024]{1,0:T(1,128)} %param.17) | copy-start | bytes 12292
  113.8 349.1 %all-gather.17.cloned.1.call-start = ((), (), s32[]{:S(2)}) async-start(), calls=%async_computation.11 | async-start | bytes 3686400 | tf_op jit(solution)/shard_map/all_gather | solution.py:182
  116.5 336.3 %copy-start.10 = (bf16[128,1600]{0,1:T(8,128)(2,1)}, bf16[128,1600]{0,1:T(8,128)(2,1)S(1)}, u32[]{:S(2)}) copy-start(bf16[128,1600]{0,1:T(8,128)(2,1)S(1)} %get-tuple-element.97) | copy-start | bytes 1228804
  116.5 354.7 %all-gather.11.cloned.1.call-start = ((), (), s32[]{:S(2)}) async-start(), calls=%async_computation.7 | async-start | bytes 5990400 | tf_op jit(solution)/shard_map/all_gather | solution.py:196
  117.1 383.1 %all-gather.13.cloned.1.call-start = ((), (), s32[]{:S(2)}) async-start(), calls=%async_computation.8 | async-start | bytes 23961600 | tf_op jit(solution)/shard_map/all_gather | solution.py:202
  117.7 435.2 %all-gather.15.cloned.1.call-start = ((), (), s32[]{:S(2)}) async-start(), calls=%async_computation.9 | async-start | bytes 23040000 | tf_op jit(solution)/shard_map/all_gather | solution.py:211
  118.3 675.8 %reduce-scatter.21.cloned.1.call-start = ((), (), s32[]{:S(2)}) async-start(), calls=%async_computation.14 | async-start | bytes 3833856
  118.3 79.5 %collective-permute-start = (bf16[200,6400]{1,0:T(8,128)(2,1)S(1)}, bf16[200,6400]{1,0:T(8,128)(2,1)}, u32[]{:S(2)}, u32[]{:S(2)}) collective-permute-start(bf16[200,6400]{1,0:T(8,128)(2,1)S(1)} %copy-done.2), channel_id=1, source_target_pairs={{0,4},{4,8},{8,12},{12,16},{16,20},{20,24},{24,28},{28,0},{1,5},{5... | collective-permute-start | bytes 7680008 | tf_op jit(solution)/shard_map/ppermute | solution.py:18
  118.6 82.2 %collective-permute-start.1 = (bf16[200,6400]{1,0:T(8,128)(2,1)S(1)}, bf16[200,6400]{1,0:T(8,128)(2,1)}, u32[]{:S(2)}, u32[]{:S(2)}) collective-permute-start(bf16[200,6400]{1,0:T(8,128)(2,1)S(1)} %copy-done.2), channel_id=1, source_target_pairs={{0,28},{4,0},{8,4},{12,8},{16,12},{20,16},{24,20},{28,24},{1,29},{... | collective-permute-start | bytes 7680008 | tf_op jit(solution)/shard_map/ppermute | solution.py:21
  197.9 81.3 %collective-permute-start.2 = (bf16[200,6400]{1,0:T(8,128)(2,1)}, bf16[200,6400]{1,0:T(8,128)(2,1)}, u32[]{:S(2)}, u32[]{:S(2)}) collective-permute-start(bf16[200,6400]{1,0:T(8,128)(2,1)} %collective-permute-done), channel_id=1, source_target_pairs={{0,4},{4,8},{8,12},{12,16},{16,20},{20,24},{24,28},{28,0},{1,5},{5... | collective-permute-start | bytes 7680008 | tf_op jit(solution)/shard_map/ppermute | solution.py:18
  200.8 86.3 %collective-permute-start.3 = (bf16[200,6400]{1,0:T(8,128)(2,1)}, bf16[200,6400]{1,0:T(8,128)(2,1)S(1)}, u32[]{:S(2)}, u32[]{:S(2)}) collective-permute-start(bf16[200,6400]{1,0:T(8,128)(2,1)} %collective-permute-done.1), channel_id=1, source_target_pairs={{0,28},{4,0},{8,4},{12,8},{16,12},{20,16},{24,20},{28,24},{1,29},{... | collective-permute-start | bytes 7680008 | tf_op jit(solution)/shard_map/ppermute | solution.py:21
  279.2 98.8 %collective-permute-start.4 = (bf16[200,6400]{1,0:T(8,128)(2,1)}, bf16[200,6400]{1,0:T(8,128)(2,1)S(1)}, u32[]{:S(2)}, u32[]{:S(2)}) collective-permute-start(bf16[200,6400]{1,0:T(8,128)(2,1)} %collective-permute-done.2), channel_id=1, source_target_pairs={{0,4},{4,8},{8,12},{12,16},{16,20},{20,24},{24,28},{28,0},{1,5},{5... | collective-permute-start | bytes 7680008 | tf_op jit(solution)/shard_map/ppermute | solution.py:18
  287.1 102.5 %collective-permute-start.5 = (bf16[200,6400]{1,0:T(8,128)(2,1)S(1)}, bf16[200,6400]{1,0:T(8,128)(2,1)S(1)}, u32[]{:S(2)}, u32[]{:S(2)}) collective-permute-start(bf16[200,6400]{1,0:T(8,128)(2,1)S(1)} %collective-permute-done.3), channel_id=1, source_target_pairs={{0,28},{4,0},{8,4},{12,8},{16,12},{20,16},{24,20},{28,24},{1,29},{... | collective-permute-start | bytes 7680008 | tf_op jit(solution)/shard_map/ppermute | solution.py:21
  378.1 73.1 %collective-permute-start.6 = (bf16[200,6400]{1,0:T(8,128)(2,1)S(1)}, bf16[200,6400]{1,0:T(8,128)(2,1)S(1)}, u32[]{:S(2)}, u32[]{:S(2)}) collective-permute-start(bf16[200,6400]{1,0:T(8,128)(2,1)S(1)} %collective-permute-done.4), channel_id=1, source_target_pairs={{0,4},{4,8},{8,12},{12,16},{16,20},{20,24},{24,28},{28,0},{1,5},{5... | collective-permute-start | bytes 7680008 | tf_op jit(solution)/shard_map/ppermute | solution.py:18
  511.6 53.0 %copy-start.3 = (bf16[128,6400]{1,0:T(8,128)(2,1)}, bf16[128,6400]{1,0:T(8,128)(2,1)S(1)}, u32[]{:S(2)}) copy-start(bf16[128,6400]{1,0:T(8,128)(2,1)S(1)} %get-tuple-element.111) | copy-start | bytes 4915204
  595.3 202.6 %reduce-scatter.19.cloned.1.call-start = ((), (), s32[]{:S(2)}) async-start(), calls=%async_computation.13 | async-start | bytes 3833856
  659.4 997.2 %all-reduce.13.cloned.1.call-start = ((), (), s32[]{:S(2)}) async-start(), calls=%async_computation.18 | async-start | bytes 123699200
  955.9 775.3 %reduce-scatter.25.cloned.1.call-start = ((), (), s32[]{:S(2)}) async-start(), calls=%async_computation.16 | async-start | bytes 1024000
  1659.3 77.4 %reduce-scatter.23.cloned.1.call-start = ((), (), s32[]{:S(2)}) async-start(), calls=%async_computation.15 | async-start | bytes 3072000
  1666.4 134.3 %reduce-scatter.27.cloned.1.call-start = ((), (), s32[]{:S(2)}) async-start(), calls=%async_computation.17 | async-start | bytes 4096000
  1678.4 180.8 %reduce-scatter.17.cloned.1.call-start = ((), (), s32[]{:S(2)}) async-start(), calls=%async_computation.10 | async-start | bytes 3584000 | tf_op jit(solution)/shard_map/reduce_scatter | solution.py:314
  (23 other events, 459.8 us)
Sparse Core Ops, SparseCore 0:
  9.9 88.1 all-gather.8
  113.9 45.9 all-gather.18
  162.3 43.3 all-gather.16
  207.5 62.7 all-gather.10
  272.1 172.7 all-gather.12
  446.6 106.2 all-gather.14
  595.4 47.4 reduce-scatter.20
  659.6 47.2 reduce-scatter.18
  956.0 700.5 all-reduce.12
  1659.4 23.7 reduce-scatter.24
  1685.5 51.1 reduce-scatter.22
  1738.8 61.8 reduce-scatter.26
  1803.0 56.2 reduce-scatter.16
